TPU v7x, 256 devices: a whole 4x4x8 slice. The times are simulated.
256 devices in a mesh: sec: 4 (over y), comp: 64 (over x, z, core).
Axes of the slice: x: 4, y: 4, z: 8, core: 2. Of those that a mesh axis runs over, the one named last changes fastest.
Arguments:
- spectrum: float32 [96, 384, 1152], P('sec', 'comp'), may hold values from 0.05 to 2
- land: int32 [96, 384], P('sec', 'comp'), may hold values 0 or 1
- currents: float32 [2, 96, 384], P(None, 'sec', 'comp'), may hold values from -0.2 to 0.2
- group_courant: float32 [32], replicated, may hold values from 0.05 to 0.4
- w_gate: bfloat16 [1152, 1152], replicated, may hold values from -0.1875 to 0.1875
- w_up: bfloat16 [1152, 1152], replicated, may hold values from -0.1875 to 0.1875
- w_down: bfloat16 [1152, 1152], replicated, may hold values from -0.1875 to 0.1875
- stokes_profile: bfloat16 [1152, 80], replicated, may hold values from -0.1875 to 0.1875
- ocean_vel: float32 [2, 40, 96, 384], P(None, None, 'sec', 'comp'), may hold values from -3 to 3
- mixing: float32 [40], replicated, may hold values from 0.05 to 0.3
Outputs:
- spectrum_next: float32 [96, 384, 1152], P('sec', 'comp')
- ocean_next: float32 [2, 40, 96, 384], P(None, None, 'sec', 'comp')
Inputs may be any that keep to these rules, and one draw needn't show every extreme that they name: 1 marks a sea point, 0 a land point.
All inputs are finite; a program needn't handle non-finite values. No bound on the sum of `land` on one device may be relied on, other than what follows from the above.
Results may differ from a plain program's by a relative error of at most 0.002.
Values sent between devices are 32-bit elements; how exact they have to be, the bound alone decides.
No kernel may reach another device: no remote copies, remote signals or barrier semaphores. Data moves between devices by JAX's collectives and lax.ppermute only.
A program may use at most 128 MiB of HBM per device.

v0:
```python
import functools
import math

import jax
import jax.numpy as jnp
from jax import lax
from jax.experimental import pallas as pl
from jax.experimental.pallas import tpu as pltpu
from jax.sharding import PartitionSpec as P


DIRS = 36
FREQS = 32
K = DIRS * FREQS
LAYERS = 40
SUBSTEPS = 4
STEPS = 3
HALO = SUBSTEPS
FAR = STEPS * HALO
OWN = 6
EXT = OWN + 2 * HALO
LANES = 128
FULL = K + LANES
WET = 80
FLOW = 82
CHUNK = 384
HALVES = ((0, 640), (640, 512))


def shrink(x, rows):
    if rows == 48:
        return jnp.concatenate([x[:32], x[40:]], axis=0)
    if rows == 40:
        low = lax.broadcasted_iota(jnp.int32, (8, x.shape[1]), 0) < 4
        return jnp.concatenate([x[:24], jnp.where(low, x[24:32], x[32:])], axis=0)
    return x[:24]


def wide(x, lane):
    return jnp.broadcast_to(x[:, lane : lane + 1], (x.shape[0], LANES))


def pack_aux(cols, sources):
    tiles = cols[0].shape[0] // 8
    lane = lax.broadcasted_iota(jnp.int32, (8, LANES), 1)
    out = jnp.zeros((8, LANES), jnp.float32)
    for c, col in enumerate(cols):
        for t in range(tiles):
            part = col[8 * t : 8 * t + 8]
            first = 3 * (c * tiles + t)
            for k, source in enumerate(sources):
                out = jnp.where(lane == first + k, wide(part, source), out)
    return out


def fill_messages(state, outs, rows):
    for side, first in ((0, 2), (1, 0)):
        for half, (start, width) in enumerate(HALVES):
            for c in range(HALO):
                outs[2 * side + half][c * rows : (c + 1) * rows, :] = state[first + c, :, start : start + width]


def message_shapes(rows):
    sizes = [(HALO * rows + (0 if half else 8), width) for half, (_, width) in enumerate(HALVES)]
    return sizes * 2


def enter(spec, land, flow, ocean, state, low, high, square):
    rows = spec.shape[1]
    lane = lax.broadcasted_iota(jnp.int32, (rows, LANES), 1)
    square[...] = jnp.zeros_like(square)
    square[:OWN, :rows] = land[...].astype(jnp.float32)
    for c in range(OWN):
        square[8 + c : 9 + c, :rows] = flow[c, 0:1]
        square[16 + c : 17 + c, :rows] = flow[c, 1:2]
    points = square[...].T[:rows]
    for c in range(OWN):
        state[c, :, :K] = spec[c] * points[:, c : c + 1]
        x = jnp.where(
            lane < 2 * LAYERS + 2,
            wide(points, c),
            jnp.where(lane == FLOW, wide(points, 8 + c), wide(points, 16 + c)),
        )
        state[c, :, K:] = x
        state[c, :, K : K + LAYERS] = ocean[0, c]
        state[c, :, K + LAYERS : K + 2 * LAYERS] = ocean[1, c]
        at = pl.ds(c * FAR, FAR)
        low[at] = state[c, rows - FAR :]
        high[at] = state[c, :FAR]


def pack_own(state, east, west):
    rows = state.shape[1]
    for c in range(HALO):
        east[c * rows : (c + 1) * rows] = state[2 + c, :, :K]
        west[c * rows : (c + 1) * rows] = state[c, :, :K]


def pack_far(own, low, high, far, *outs):
    band = lax.axis_index("sec")
    keep_low = jnp.where(band > 0, 1.0, 0.0)
    keep_high = jnp.where(band < lax.axis_size("sec") - 1, 1.0, 0.0)
    for c in range(OWN):
        at = pl.ds(c * FAR, FAR)
        far[c, :FAR] = high[at] * keep_high
        far[c, FAR:] = low[at] * keep_low
    fill_messages(far, outs, 2 * FAR)
    both = [jnp.concatenate([own[c, :, K:], far[c, :, K:]], axis=0) for c in range(OWN)]
    for side, first in ((0, 2), (1, 0)):
        tile = pack_aux(both[first : first + HALO], (FLOW, FLOW + 1, WET))
        outs[2 * side][HALO * 2 * FAR :, :LANES] = tile


def advect(half, rows, first, states, from_w, from_e, aux_w, aux_e, speeds, out, out_first, scratch):
    s0, s1, wet, gx, gy, field = scratch
    tiles = rows // 8
    start, width = HALVES[half]
    for c in range(EXT):
        if HALO <= c < HALO + OWN:
            x = jnp.concatenate([piece[c - HALO, :, K:] for piece in states], axis=0)
            wet[c] = wide(x, WET)
            y = x if first else 0.2 * jnp.tanh(x)
            s0[c] = wide(y, FLOW if first else 0)
            s1[c] = wide(y, FLOW + 1 if first else LAYERS)
        else:
            ref, k = (aux_w, c) if c < HALO else (aux_e, c - HALO - OWN)
            x = ref[ref.shape[0] - 8 :, :LANES]
            for t in range(tiles):
                lane = 3 * (k * tiles + t)
                at = pl.ds(8 * t, 8)
                s0[c, at] = wide(x, lane)
                s1[c, at] = wide(x, lane + 1)
                wet[c, at] = wide(x, lane + 2)

    def store(b, c, base, x):
        n = x.shape[0]
        field[b, c, 8 + base : 8 + base + n] = x
        if base == 0:
            field[b, c, 8 + rows :] = x[:8]
        if base + n == rows:
            field[b, c, :8] = x[n - 8 :]

    def body(j, _):
        here_at = pl.ds(pl.multiple_of(j * LANES, LANES), LANES)
        spec_at = pl.ds(pl.multiple_of(start + j * LANES, LANES), LANES)
        along_x = speeds[0:1, spec_at]
        along_y = speeds[1:2, spec_at]
        for c in range(EXT):
            base = 0
            for p, piece in enumerate(states):
                n = piece.shape[1]
                if HALO <= c < HALO + OWN:
                    x = piece[c - HALO, :, spec_at]
                else:
                    ref, k = (from_w[p], c) if c < HALO else (from_e[p], c - HALO - OWN)
                    x = ref[k * n : (k + 1) * n, spec_at if ref.shape[1] == K else here_at]
                store(1, c, base, x)
                base += n
        for c in range(1, EXT - 1):
            w = wet[c]
            gx[c] = w * (along_x + s0[c])
            gy[c] = w * (along_y + s1[c])
        for sub in range(SUBSTEPS):
            b = (sub + 1) % 2
            mid = pl.ds(8, rows)
            before = field[b, sub, mid]
            here = field[b, sub + 1, mid]
            for c in range(sub + 1, EXT - sub - 1):
                after = field[b, c + 1, mid]
                x, y = gx[c], gy[c]
                from_x = jnp.where(x > 0.0, before, after)
                from_y = jnp.where(y > 0.0, field[b, c, 7 : 7 + rows], field[b, c, 9 : 9 + rows])
                new = here - jnp.abs(x) * (here - from_x) - jnp.abs(y) * (here - from_y)
                if sub < SUBSTEPS - 1:
                    store(sub % 2, c, 0, new)
                else:
                    at = pl.ds(pl.multiple_of(out_first + j * LANES, LANES), LANES)
                    out[c - HALO, :, at] = shrink(new, rows)
                before, here = here, after
        return 0

    lax.fori_loop(0, width // LANES, body, 0)


def first_kernel(rows, pieces, *refs):
    refs = list(refs)
    take = lambda n: [refs.pop(0) for _ in range(n)]
    states, from_w, from_e, (speeds, out) = take(pieces), take(pieces), take(pieces), take(2)
    advect(0, rows, pieces > 1, states, from_w, from_e, from_w[-1], from_e[-1], speeds, out, 0, refs)


def second_kernel(rows, pieces, last, *refs):
    refs = list(refs)
    take = lambda n: [refs.pop(0) for _ in range(n)]
    states, from_w, from_e = take(pieces), take(pieces), take(pieces)
    (aux_w, aux_e, speeds, done, rate, mixing, w_gate, w_up, w_down, profile, state_out) = take(11)
    if last:
        (ocean_out,) = take(1)
    else:
        messages = take(4)
    act, hidden = take(2)
    split = HALVES[1][0]
    fewer = rows - 2 * HALO
    advect(1, rows, pieces > 1, states, from_w, from_e, aux_w, aux_e, speeds, state_out, split, refs)
    wet = refs[2]

    for c in range(OWN):
        at = pl.ds(c * fewer, fewer)
        act[at, :split] = done[c].astype(jnp.bfloat16)
        act[at, split:] = state_out[c, :, split:K].astype(jnp.bfloat16)
    for n in range(0, K, CHUNK):
        a = act[...]
        gate = jnp.dot(a, w_gate[:, n : n + CHUNK], preferred_element_type=jnp.float32)
        up = jnp.dot(a, w_up[:, n : n + CHUNK], preferred_element_type=jnp.float32)
        hidden[:, n : n + CHUNK] = (jax.nn.silu(gate) * up).astype(jnp.bfloat16)
    for n, size in ((0, 384), (384, 256), (640, 256), (896, 256)):
        source = jnp.dot(hidden[...], w_down[:, n : n + size], preferred_element_type=jnp.float32)
        for c in range(OWN):
            mask = shrink(wet[c + HALO], rows)[:, :1]
            at = pl.ds(c * fewer, fewer)
            old = done[c, :, n : n + size] if n < split else state_out[c, :, n : n + size]
            fresh = mask * (old + source[c * fewer : (c + 1) * fewer])
            state_out[c, :, n : n + size] = fresh
            act[at, n : n + size] = fresh.astype(jnp.bfloat16)
    stokes = jnp.dot(act[...], profile[...], preferred_element_type=jnp.float32)

    lane = lax.broadcasted_iota(jnp.int32, (fewer, LANES), 1)
    east = lane < LAYERS
    kappa = mixing[...]
    speed = rate[...]
    for r in range(rate.shape[0], rows - 1, -2 * HALO):
        speed = shrink(speed, r)
    surf = []
    for c in range(OWN):
        v = shrink(jnp.concatenate([piece[c, :, K:] for piece in states], axis=0), rows)
        lower = jnp.where((lane == 0) | (lane == LAYERS), v, pltpu.roll(v, 1, 1))
        upper = jnp.where((lane == LAYERS - 1) | (lane == 2 * LAYERS - 1), v, pltpu.roll(v, LANES - 1, 1))
        lap = lower - 2.0 * v + upper
        moved = v + stokes[c * fewer : (c + 1) * fewer]
        other = jnp.where(east, pltpu.roll(moved, LANES - LAYERS, 1), -pltpu.roll(moved, LAYERS, 1))
        new = wide(v, WET) * (v + kappa * lap + speed * other)
        if last:
            ocean_out[0, c] = new[:, :LAYERS]
            ocean_out[1, c] = new[:, LAYERS : 2 * LAYERS]
        else:
            new = jnp.where(lane < 2 * LAYERS, new, v)
            state_out[c, :, K:] = new
            surf.append(jnp.where(lane < 2 * LAYERS, 0.2 * jnp.tanh(new), v))
    if not last:
        fill_messages(state_out, messages, fewer)
        for side, first in ((0, 2), (1, 0)):
            tile = pack_aux(surf[first : first + HALO], (0, LAYERS, WET))
            messages[2 * side][HALO * fewer :, :LANES] = tile


def kernel_call(body, outs, scratch, *args, flops=0):
    block = pl.BlockSpec(memory_space=pltpu.VMEM)
    return pl.pallas_call(
        body,
        out_shape=[jax.ShapeDtypeStruct(shape, jnp.float32) for shape in outs],
        in_specs=[block] * len(args),
        out_specs=[block] * len(outs),
        scratch_shapes=scratch,
        compiler_params=pltpu.CompilerParams(vmem_limit_bytes=14 << 20),
        cost_estimate=pl.CostEstimate(flops=flops, bytes_accessed=1 << 20, transcendentals=0),
    )(*args)


def shards(
    spectrum, land, currents, group_courant, w_gate, w_up, w_down, stokes_profile, ocean_vel, mixing
):
    rows, columns, _ = spectrum.shape
    bands, sectors = lax.axis_size("sec"), lax.axis_size("comp")
    band = lax.axis_index("sec")
    up = [(i, (i + 1) % bands) for i in range(bands)]
    down = [(b, a) for a, b in up]
    east = [(i, (i + 1) % sectors) for i in range(sectors)]
    west = [(b, a) for a, b in east]

    def send_columns(messages):
        half = len(messages) // 2
        from_w = [lax.ppermute(m, "comp", east) for m in messages[:half]]
        from_e = [lax.ppermute(m, "comp", west) for m in messages[half:]]
        return [from_w[0], from_w[-1]], [from_e[0], from_e[-1]]

    edge = (columns * FAR, FULL)
    state, low, high = kernel_call(
        enter,
        [(columns, rows, FULL), edge, edge],
        [pltpu.VMEM((LANES, LANES), jnp.float32)],
        spectrum.transpose(1, 0, 2), land.T, currents.transpose(2, 0, 1), ocean_vel.transpose(0, 3, 2, 1),
    )
    low = lax.ppermute(low, "sec", up)
    high = lax.ppermute(high, "sec", down)
    own = send_columns(kernel_call(pack_own, [(HALO * rows, K)] * 2, [], state))

    tall = rows + 2 * FAR
    places = jnp.concatenate([jnp.arange(rows + FAR), jnp.arange(-FAR, 0)])
    places = (band * rows + places).astype(jnp.float32)
    rate = 0.5 * jnp.sin((places + 0.5) * (math.pi / (rows * bands)) - math.pi / 2)
    rate = jnp.broadcast_to(rate[:, None], (tall, LANES))

    theta = 2.0 * math.pi * (jnp.arange(DIRS).astype(jnp.float32) + 0.5) / DIRS
    speed = jnp.repeat(group_courant, DIRS)
    speeds = jnp.stack([speed * jnp.tile(jnp.cos(theta), FREQS), speed * jnp.tile(jnp.sin(theta), FREQS)])
    speeds = jnp.pad(speeds, ((0, 6), (0, 0)))
    kappa = jnp.pad(jnp.concatenate([mixing, mixing]), (0, LANES - 2 * LAYERS))[None, :]
    profile = jnp.pad(stokes_profile, ((0, 0), (0, LANES - 2 * LAYERS)))

    far, *messages = kernel_call(
        pack_far, [(columns, 2 * FAR, FULL), *message_shapes(2 * FAR)], [], state, low, high
    )
    states = [state, far]
    arrived = [own, send_columns(messages)]
    for step in range(STEPS):
        last = step == STEPS - 1
        fewer = tall - 2 * HALO
        pieces = len(states)
        plane = (EXT, tall, LANES)
        scratch = [pltpu.VMEM(plane, jnp.float32)] * 5 + [
            pltpu.VMEM((2, EXT, tall + 16, LANES), jnp.float32),
        ]
        matmul = [pltpu.VMEM((columns * fewer, K), jnp.bfloat16)] * 2
        from_w = [[a[0][half] for a in arrived] for half in range(2)]
        from_e = [[a[1][half] for a in arrived] for half in range(2)]
        (done,) = kernel_call(
            functools.partial(first_kernel, tall, pieces),
            [(columns, fewer, HALVES[0][1])],
            scratch,
            *states, *from_w[0], *from_e[0], speeds,
            flops=1 << 31,
        )
        if last:
            outs = [(columns, fewer, K), (2, columns, fewer, LAYERS)]
        else:
            outs = [(columns, fewer, FULL), *message_shapes(fewer)]
        result = kernel_call(
            functools.partial(second_kernel, tall, pieces, last),
            outs,
            matmul + scratch,
            *states, *from_w[1], *from_e[1], from_w[0][-1], from_e[0][-1],
            speeds, done, rate, kappa, w_gate, w_up, w_down, profile,
            flops=1 << 32,
        )
        if not last:
            states, arrived = [result[0]], [send_columns(result[1:])]
        tall = fewer
    spec, ocean = result
    return spec.transpose(1, 0, 2), ocean.transpose(0, 3, 2, 1)


def solution(mesh):
    return jax.shard_map(
        shards,
        mesh=mesh,
        in_specs=(
            P("sec", "comp", None),
            P("sec", "comp"),
            P(None, "sec", "comp"),
            P(),
            P(),
            P(),
            P(),
            P(),
            P(None, None, "sec", "comp"),
            P(),
        ),
        out_specs=(P("sec", "comp", None), P(None, None, "sec", "comp")),
        check_vma=False,
    )
```

profile of v0, /device:TPU:24, one launch (start us, length us, event | category | flops | bytes accessed | tf_op | source)
XLA Modules:
  0.0 83.8 jit_solution(738932958111814785)
XLA Ops:
  0.6 1.1 %copy-done = f32[24,6,1152]{2,0,1:T(8,128)S(1)} copy-done((f32[24,6,1152]{2,0,1:T(8,128)S(1)}, f32[24,6,1152]{2,0,1:T(8,128)}, u32[]{:S(2)}) %copy-start) | copy-done | bytes 663576
  1.7 0.9 %copy-done.1 = f32[2,40,24,6]{1,2,3,0:T(8,128)S(1)} copy-done((f32[2,40,24,6]{1,2,3,0:T(8,128)S(1)}, f32[2,40,24,6]{1,2,3,0:T(8,128)}, u32[]{:S(2)}) %copy-start.1) | copy-done | bytes 46104
  2.6 0.7 copy-done.2
  3.3 0.7 copy-done.3
  4.0 0.3 shard_map.113
  4.3 2.0 %collective-permute-start = (f32[72,1280]{1,0:T(8,128)S(1)}, f32[72,1280]{1,0:T(8,128)S(1)}, u32[]{:S(2)}, u32[]{:S(2)}) collective-permute-start(f32[72,1280]{1,0:T(8,128)S(1)} %get-tuple-element.25), channel_id=1, source_target_pairs={{0,64},{64,128},{128,192},{192,0},{1,65},{65,129},{129,193},{193,1... | collective-permute-start | bytes 1105928 | tf_op jit(solution)/shard_map/ppermute | solution.py:293
  6.3 0.1 collective-permute-start.1
  6.4 0.8 shard_map.115
  7.3 0.0 collective-permute-start.2
  7.3 6.9 %collective-permute-start.4 = (f32[96,1152]{1,0:T(8,128)S(1)}, f32[96,1152]{1,0:T(8,128)S(1)}, u32[]{:S(2)}, u32[]{:S(2)}) collective-permute-start(f32[96,1152]{1,0:T(8,128)S(1)} %get-tuple-element.30), channel_id=1, source_target_pairs={{1,0},{2,1},{3,2},{4,3},{5,4},{6,5},{7,6},{8,7},{9,8},{10,9},{11,1... | collective-permute-start | bytes 1327112 | tf_op jit(solution)/shard_map/ppermute | solution.py:283
  14.2 1.3 %broadcast_multiply_fusion.1 = (f32[32,36]{1,0:T(8,128)}, f32[32,36]{1,0:T(8,128)}) fusion(f32[36]{0:T(128)S(1)} %get-tuple-element.49, f32[32]{0:T(128)} %param.13, f32[36]{0:T(128)S(1)} %get-tuple-element.48), kind=kLoop, calls=%fused_computation.3 | loop fusion | flops 2304 | bytes 9632 | tf_op jit(solution)/shard_map/mul | solution.py:305
  15.6 0.8 fusion.1.refs_11_.refs_8_
  16.4 0.0 collective-permute-done.low
  16.4 0.0 collective-permute-done.1.high
  16.4 1.1 %shard_map.114 = (f32[6,24,1280]{2,1,0:T(8,128)S(1)}, f32[104,640]{1,0:T(8,128)}, f32[96,512]{1,0:T(8,128)S(1)}, f32[104,640]{1,0:T(8,128)}, f32[96,512]{1,0:T(8,128)S(1)}) custom-call(f32[6,24,1280]{2,1,0:T(8,128)S(1)} %get-tuple-element.24.own.state.refs_0_, f32[72,1280]{1,0:T(8,128)S(1)} %collective-permute-done.low, ...), custom_call_target="tpu_custom_call" | custom-call | bytes 1048576 | tf_op jit(solution)/shard_map/pallas_call | solution.py:258
  17.5 0.7 copy-done.9
  18.2 0.7 copy-done.10
  18.9 6.1 %collective-permute-start.7 = (f32[104,640]{1,0:T(8,128)}, f32[104,640]{1,0:T(8,128)S(1)}, u32[]{:S(2)}, u32[]{:S(2)}) collective-permute-start(f32[104,640]{1,0:T(8,128)} %get-tuple-element.33), channel_id=1, source_target_pairs={{1,0},{2,1},{3,2},{4,3},{5,4},{6,5},{7,6},{8,7},{9,8},{10,9},{11,1... | collective-permute-start | bytes 798728 | tf_op jit(solution)/shard_map/ppermute | solution.py:283
  25.0 0.1 sine_multiply_fusion
  25.1 0.8 mul.49
  25.9 0.8 mul.51
  26.8 1.8 %copy.12 = bf16[1152,80]{1,0:T(8,128)(2,1)} copy(bf16[1152,80]{0,1:T(8,128)(2,1)} %param.17) | data formatting | bytes 368640 | tf_op args[7]
  28.6 1.0 %pad.14.refs_15_.refs_12_ = bf16[1152,128]{1,0:T(8,128)(2,1)S(1)} pad(bf16[1152,80]{1,0:T(8,128)(2,1)} %copy.12, bf16[]{:T(256)} %constant.27.clone.1), padding=0_0x0_48 | pad | bytes 479234 | tf_op jit(solution)/shard_map/jit(_pad)/pad | solution.py:308
  29.6 0.1 collective-permute-start.3
  29.7 5.0 %collective-permute-start.5 = (f32[96,512]{1,0:T(8,128)}, f32[96,512]{1,0:T(8,128)S(1)}, u32[]{:S(2)}, u32[]{:S(2)}) collective-permute-start(f32[96,512]{1,0:T(8,128)} %copy-done.9), channel_id=1, source_target_pairs={{1,0},{2,1},{3,2},{4,3},{5,4},{6,5},{7,6},{8,7},{9,8},{10,9},{11,1... | collective-permute-start | bytes 589832 | tf_op jit(solution)/shard_map/ppermute | solution.py:283
  34.8 0.0 copy-start.7
  34.8 0.0 copy-start.4
  34.8 0.0 copy-start.5
  34.8 0.0 copy-start.6
  34.8 2.4 %shard_map.116.refs_9_ = f32[6,40,640]{2,1,0:T(8,128)S(1)} custom-call(f32[6,24,1280]{2,1,0:T(8,128)S(1)} %get-tuple-element.24.own.state.refs_0_, f32[6,24,1280]{2,1,0:T(8,128)S(1)} %get-tuple-element.27.refs_1_, f32[96,1152]{1,0:T(8,128)S(1)} %collective-permute-done.2.refs_2_, f32[104,640]{1,0:T(8,128)S(1)} %collective-permute-done.6.refs_3_.refs_6_, ...), custom_call_target="tpu_custom_call" | custom-call | flops 2147483648 | bytes 1048576 | tf_op jit(solution)/shard_map/pallas_call | solution.py:258
  37.2 1.1 %collective-permute-done.3.refs_3_ = f32[96,512]{1,0:T(8,128)S(1)} collective-permute-done((f32[96,512]{1,0:T(8,128)}, f32[96,512]{1,0:T(8,128)S(1)}, u32[]{:S(2)}, u32[]{:S(2)}) %collective-permute-start.3) | collective-permute-done | bytes 196640 | tf_op jit(solution)/shard_map/ppermute | solution.py:282
  38.3 0.1 broadcast_in_dim.13.refs_10_.refs_7_
  38.4 0.0 copy-start.8
  38.4 0.9 %copy-done.8 = f32[104,640]{1,0:T(8,128)S(1)} copy-done((f32[104,640]{1,0:T(8,128)S(1)}, f32[104,640]{1,0:T(8,128)}, u32[]{:S(2)}) %copy-start.8) | copy-done | bytes 266264
  39.4 5.6 %shard_map.117 = (f32[6,40,1280]{2,1,0:T(8,128)S(1)}, f32[168,640]{1,0:T(8,128)S(1)}, f32[160,512]{1,0:T(8,128)S(1)}, f32[168,640]{1,0:T(8,128)S(1)}, f32[160,512]{1,0:T(8,128)S(1)}) custom-call(f32[6,24,1280]{2,1,0:T(8,128)S(1)} %get-tuple-element.24.own.state.refs_0_, f32[6,24,1280]{2,1,0:T(8,128)S(1)} %get-tuple-element.27.refs_1_, ...), custom_call_target="tpu_custom_call" | custom-call | flops 4294967296 | bytes 1048576 | tf_op jit(solution)/shard_map/pallas_call | solution.py:258
  45.0 0.1 collective-permute-start.10
  45.1 5.1 %collective-permute-start.11 = (f32[168,640]{1,0:T(8,128)S(1)}, f32[168,640]{1,0:T(8,128)S(1)}, u32[]{:S(2)}, u32[]{:S(2)}) collective-permute-start(f32[168,640]{1,0:T(8,128)S(1)} %get-tuple-element.38), channel_id=1, source_target_pairs={{1,0},{2,1},{3,2},{4,3},{5,4},{6,5},{7,6},{8,7},{9,8},{10,9},{11,1... | collective-permute-start | bytes 1290248 | tf_op jit(solution)/shard_map/ppermute | solution.py:283
  50.2 5.1 %collective-permute-start.9 = (f32[160,512]{1,0:T(8,128)S(1)}, f32[160,512]{1,0:T(8,128)S(1)}, u32[]{:S(2)}, u32[]{:S(2)}) collective-permute-start(f32[160,512]{1,0:T(8,128)S(1)} %get-tuple-element.36), channel_id=1, source_target_pairs={{1,0},{2,1},{3,2},{4,3},{5,4},{6,5},{7,6},{8,7},{9,8},{10,9},{11,1... | collective-permute-start | bytes 983048 | tf_op jit(solution)/shard_map/ppermute | solution.py:283
  55.3 0.7 collective-permute-done.10.refs_1_.refs_3_
  56.0 2.0 %shard_map.118.refs_6_ = f32[6,32,640]{2,1,0:T(8,128)S(1)} custom-call(f32[6,40,1280]{2,1,0:T(8,128)S(1)} %get-tuple-element.34.refs_0_, f32[168,640]{1,0:T(8,128)S(1)} %collective-permute-done.10.refs_1_.refs_3_, f32[168,640]{1,0:T(8,128)S(1)} %collective-permute-done.11.refs_2_.refs_4_, f32[8,1152]{1,0:T(8,128)S(1)} %select_maximum_fusion.refs_6_.refs_8_.refs_3_.refs_5_), custom_call_target="tpu_custom_call" | custom-call | flops 2147483648 | bytes 1048576 | tf_op jit(solution)/shard_map/pallas_call | solution.py:258
  58.1 2.0 %collective-permute-done.8.refs_1_ = f32[160,512]{1,0:T(8,128)S(1)} collective-permute-done((f32[160,512]{1,0:T(8,128)S(1)}, f32[160,512]{1,0:T(8,128)S(1)}, u32[]{:S(2)}, u32[]{:S(2)}) %collective-permute-start.8) | collective-permute-done | bytes 327712 | tf_op jit(solution)/shard_map/ppermute | solution.py:282
  60.1 4.7 %shard_map.119 = (f32[6,32,1280]{2,1,0:T(8,128)S(1)}, f32[136,640]{1,0:T(8,128)S(1)}, f32[128,512]{1,0:T(8,128)S(1)}, f32[136,640]{1,0:T(8,128)S(1)}, f32[128,512]{1,0:T(8,128)S(1)}) custom-call(f32[6,40,1280]{2,1,0:T(8,128)S(1)} %get-tuple-element.34.refs_0_, f32[160,512]{1,0:T(8,128)S(1)} %collective-permute-done.8.refs_1_, ...), custom_call_target="tpu_custom_call" | custom-call | flops 4294967296 | bytes 1048576 | tf_op jit(solution)/shard_map/pallas_call | solution.py:258
  64.8 0.3 collective-permute-start.14
  65.1 5.1 %collective-permute-start.15 = (f32[136,640]{1,0:T(8,128)S(1)}, f32[136,640]{1,0:T(8,128)S(1)}, u32[]{:S(2)}, u32[]{:S(2)}) collective-permute-start(f32[136,640]{1,0:T(8,128)S(1)} %get-tuple-element.43), channel_id=1, source_target_pairs={{1,0},{2,1},{3,2},{4,3},{5,4},{6,5},{7,6},{8,7},{9,8},{10,9},{11,1... | collective-permute-start | bytes 1044488 | tf_op jit(solution)/shard_map/ppermute | solution.py:283
  70.2 5.1 %collective-permute-start.13 = (f32[128,512]{1,0:T(8,128)S(1)}, f32[128,512]{1,0:T(8,128)S(1)}, u32[]{:S(2)}, u32[]{:S(2)}) collective-permute-start(f32[128,512]{1,0:T(8,128)S(1)} %get-tuple-element.41), channel_id=1, source_target_pairs={{1,0},{2,1},{3,2},{4,3},{5,4},{6,5},{7,6},{8,7},{9,8},{10,9},{11,1... | collective-permute-start | bytes 786440 | tf_op jit(solution)/shard_map/ppermute | solution.py:283
  75.3 1.6 %shard_map.120.refs_6_ = f32[6,24,640]{2,1,0:T(8,128)S(1)} custom-call(f32[6,32,1280]{2,1,0:T(8,128)S(1)} %get-tuple-element.39.refs_0_, f32[136,640]{1,0:T(8,128)S(1)} %collective-permute-done.14.refs_1_.refs_3_, f32[136,640]{1,0:T(8,128)S(1)} %collective-permute-done.15.refs_2_.refs_4_, f32[8,1152]{1,0:T(8,128)S(1)} %select_maximum_fusion.refs_6_.refs_8_.refs_3_.refs_5_), custom_call_target="tpu_custom_call" | custom-call | flops 2147483648 | bytes 1048576 | tf_op jit(solution)/shard_map/pallas_call | solution.py:258
  76.9 2.5 %collective-permute-done.12.refs_1_ = f32[128,512]{1,0:T(8,128)S(1)} collective-permute-done((f32[128,512]{1,0:T(8,128)S(1)}, f32[128,512]{1,0:T(8,128)S(1)}, u32[]{:S(2)}, u32[]{:S(2)}) %collective-permute-start.12) | collective-permute-done | bytes 262176 | tf_op jit(solution)/shard_map/ppermute | solution.py:282
  79.3 4.5 %shard_map.121 = (f32[6,24,1152]{2,1,0:T(8,128)}, f32[2,6,24,40]{3,2,1,0:T(8,128)}) custom-call(f32[6,32,1280]{2,1,0:T(8,128)S(1)} %get-tuple-element.39.refs_0_, f32[128,512]{1,0:T(8,128)S(1)} %collective-permute-done.12.refs_1_, f32[128,512]{1,0:T(8,128)S(1)} %collective-permute-done.13.refs_2_, f32[136,640]{1,0:T(8,128)S(1)} %collective-permute-done.14.refs_1_.refs_3_, ...), custom_call_target="tpu_custom_call" | custom-call | flops 4294967296 | bytes 1048576 | tf_op jit(solution)/shard_map/pallas_call | solution.py:258
  (27 shorter events, 0.1 us)
Async XLA Ops:
  0.6 1.1 %copy-start = (f32[24,6,1152]{2,0,1:T(8,128)S(1)}, f32[24,6,1152]{2,0,1:T(8,128)}, u32[]{:S(2)}) copy-start(f32[24,6,1152]{2,0,1:T(8,128)} %param.10) | copy-start | bytes 1990660
  1.7 0.9 %copy-start.1 = (f32[2,40,24,6]{1,2,3,0:T(8,128)S(1)}, f32[2,40,24,6]{1,2,3,0:T(8,128)}, u32[]{:S(2)}) copy-start(f32[2,40,24,6]{1,2,3,0:T(8,128)} %param.18) | copy-start | bytes 138244
  2.6 0.7 copy-start.2
  3.3 0.7 copy-start.3
  4.3 12.1 %collective-permute-start = (f32[72,1280]{1,0:T(8,128)S(1)}, f32[72,1280]{1,0:T(8,128)S(1)}, u32[]{:S(2)}, u32[]{:S(2)}) collective-permute-start(f32[72,1280]{1,0:T(8,128)S(1)} %get-tuple-element.25), channel_id=1, source_target_pairs={{0,64},{64,128},{128,192},{192,0},{1,65},{65,129},{129,193},{193,1... | collective-permute-start | bytes 1105928 | tf_op jit(solution)/shard_map/ppermute | solution.py:293
  6.3 10.1 %collective-permute-start.1 = (f32[72,1280]{1,0:T(8,128)S(1)}, f32[72,1280]{1,0:T(8,128)S(1)}, u32[]{:S(2)}, u32[]{:S(2)}) collective-permute-start(f32[72,1280]{1,0:T(8,128)S(1)} %get-tuple-element.26), channel_id=1, source_target_pairs={{64,0},{128,64},{192,128},{0,192},{65,1},{129,65},{193,129},{1,193... | collective-permute-start | bytes 1105928 | tf_op jit(solution)/shard_map/ppermute | solution.py:294
  7.3 22.5 %collective-permute-start.2 = (f32[96,1152]{1,0:T(8,128)}, f32[96,1152]{1,0:T(8,128)S(1)}, u32[]{:S(2)}, u32[]{:S(2)}) collective-permute-start(f32[96,1152]{1,0:T(8,128)} %get-tuple-element.28), channel_id=1, source_target_pairs={{0,1},{1,2},{2,3},{3,4},{4,5},{5,6},{6,7},{7,8},{8,9},{9,10},{10,1... | collective-permute-start | bytes 1327112 | tf_op jit(solution)/shard_map/ppermute | solution.py:282
  7.3 27.5 %collective-permute-start.4 = (f32[96,1152]{1,0:T(8,128)S(1)}, f32[96,1152]{1,0:T(8,128)S(1)}, u32[]{:S(2)}, u32[]{:S(2)}) collective-permute-start(f32[96,1152]{1,0:T(8,128)S(1)} %get-tuple-element.30), channel_id=1, source_target_pairs={{1,0},{2,1},{3,2},{4,3},{5,4},{6,5},{7,6},{8,7},{9,8},{10,9},{11,1... | collective-permute-start | bytes 1327112 | tf_op jit(solution)/shard_map/ppermute | solution.py:283
  17.5 0.7 copy-start.9
  18.2 0.7 copy-start.10
  18.9 15.9 %collective-permute-start.6 = (f32[104,640]{1,0:T(8,128)}, f32[104,640]{1,0:T(8,128)S(1)}, u32[]{:S(2)}, u32[]{:S(2)}) collective-permute-start(f32[104,640]{1,0:T(8,128)} %get-tuple-element.32), channel_id=1, source_target_pairs={{0,1},{1,2},{2,3},{3,4},{4,5},{5,6},{6,7},{7,8},{8,9},{9,10},{10,1... | collective-permute-start | bytes 798728 | tf_op jit(solution)/shard_map/ppermute | solution.py:282
  18.9 15.9 %collective-permute-start.7 = (f32[104,640]{1,0:T(8,128)}, f32[104,640]{1,0:T(8,128)S(1)}, u32[]{:S(2)}, u32[]{:S(2)}) collective-permute-start(f32[104,640]{1,0:T(8,128)} %get-tuple-element.33), channel_id=1, source_target_pairs={{1,0},{2,1},{3,2},{4,3},{5,4},{6,5},{7,6},{8,7},{9,8},{10,9},{11,1... | collective-permute-start | bytes 798728 | tf_op jit(solution)/shard_map/ppermute | solution.py:283
  29.6 8.7 %collective-permute-start.3 = (f32[96,512]{1,0:T(8,128)}, f32[96,512]{1,0:T(8,128)S(1)}, u32[]{:S(2)}, u32[]{:S(2)}) collective-permute-start(f32[96,512]{1,0:T(8,128)} %copy-done.10), channel_id=1, source_target_pairs={{0,1},{1,2},{2,3},{3,4},{4,5},{5,6},{6,7},{7,8},{8,9},{9,10},{10,1... | collective-permute-start | bytes 589832 | tf_op jit(solution)/shard_map/ppermute | solution.py:282
  29.7 8.6 %collective-permute-start.5 = (f32[96,512]{1,0:T(8,128)}, f32[96,512]{1,0:T(8,128)S(1)}, u32[]{:S(2)}, u32[]{:S(2)}) collective-permute-start(f32[96,512]{1,0:T(8,128)} %copy-done.9), channel_id=1, source_target_pairs={{1,0},{2,1},{3,2},{4,3},{5,4},{6,5},{7,6},{8,7},{9,8},{10,9},{11,1... | collective-permute-start | bytes 589832 | tf_op jit(solution)/shard_map/ppermute | solution.py:283
  34.8 2.5 %copy-start.7 = (f32[104,640]{1,0:T(8,128)}, f32[104,640]{1,0:T(8,128)S(1)}, u32[]{:S(2)}) copy-start(f32[104,640]{1,0:T(8,128)S(1)} %collective-permute-done.7.refs_5_.refs_7_) | copy-start | bytes 798724
  34.8 3.6 %copy-start.4 = (bf16[1152,1152]{1,0:T(8,128)(2,1)S(1)}, bf16[1152,1152]{1,0:T(8,128)(2,1)}, u32[]{:S(2)}) copy-start(bf16[1152,1152]{1,0:T(8,128)(2,1)} %refs_9_.3) | copy-start | bytes 7962628
  34.8 3.6 %copy-start.5 = (bf16[1152,1152]{1,0:T(8,128)(2,1)S(1)}, bf16[1152,1152]{1,0:T(8,128)(2,1)}, u32[]{:S(2)}) copy-start(bf16[1152,1152]{1,0:T(8,128)(2,1)} %refs_10_.3) | copy-start | bytes 7962628
  34.8 3.6 %copy-start.6 = (bf16[1152,1152]{1,0:T(8,128)(2,1)S(1)}, bf16[1152,1152]{1,0:T(8,128)(2,1)}, u32[]{:S(2)}) copy-start(bf16[1152,1152]{1,0:T(8,128)(2,1)} %refs_11_.3) | copy-start | bytes 7962628
  38.4 1.0 %copy-start.8 = (f32[104,640]{1,0:T(8,128)S(1)}, f32[104,640]{1,0:T(8,128)}, u32[]{:S(2)}) copy-start(f32[104,640]{1,0:T(8,128)} %copy-done.7) | copy-start | bytes 798724
  45.0 11.0 %collective-permute-start.10 = (f32[168,640]{1,0:T(8,128)S(1)}, f32[168,640]{1,0:T(8,128)S(1)}, u32[]{:S(2)}, u32[]{:S(2)}) collective-permute-start(f32[168,640]{1,0:T(8,128)S(1)} %get-tuple-element.37), channel_id=1, source_target_pairs={{0,1},{1,2},{2,3},{3,4},{4,5},{5,6},{6,7},{7,8},{8,9},{9,10},{10,1... | collective-permute-start | bytes 1290248 | tf_op jit(solution)/shard_map/ppermute | solution.py:282
  45.1 10.9 %collective-permute-start.11 = (f32[168,640]{1,0:T(8,128)S(1)}, f32[168,640]{1,0:T(8,128)S(1)}, u32[]{:S(2)}, u32[]{:S(2)}) collective-permute-start(f32[168,640]{1,0:T(8,128)S(1)} %get-tuple-element.38), channel_id=1, source_target_pairs={{1,0},{2,1},{3,2},{4,3},{5,4},{6,5},{7,6},{8,7},{9,8},{10,9},{11,1... | collective-permute-start | bytes 1290248 | tf_op jit(solution)/shard_map/ppermute | solution.py:283
  50.2 9.8 %collective-permute-start.8 = (f32[160,512]{1,0:T(8,128)S(1)}, f32[160,512]{1,0:T(8,128)S(1)}, u32[]{:S(2)}, u32[]{:S(2)}) collective-permute-start(f32[160,512]{1,0:T(8,128)S(1)} %get-tuple-element.35), channel_id=1, source_target_pairs={{0,1},{1,2},{2,3},{3,4},{4,5},{5,6},{6,7},{7,8},{8,9},{9,10},{10,1... | collective-permute-start | bytes 983048 | tf_op jit(solution)/shard_map/ppermute | solution.py:282
  50.2 9.8 %collective-permute-start.9 = (f32[160,512]{1,0:T(8,128)S(1)}, f32[160,512]{1,0:T(8,128)S(1)}, u32[]{:S(2)}, u32[]{:S(2)}) collective-permute-start(f32[160,512]{1,0:T(8,128)S(1)} %get-tuple-element.36), channel_id=1, source_target_pairs={{1,0},{2,1},{3,2},{4,3},{5,4},{6,5},{7,6},{8,7},{9,8},{10,9},{11,1... | collective-permute-start | bytes 983048 | tf_op jit(solution)/shard_map/ppermute | solution.py:283
  64.8 10.5 %collective-permute-start.14 = (f32[136,640]{1,0:T(8,128)S(1)}, f32[136,640]{1,0:T(8,128)S(1)}, u32[]{:S(2)}, u32[]{:S(2)}) collective-permute-start(f32[136,640]{1,0:T(8,128)S(1)} %get-tuple-element.42), channel_id=1, source_target_pairs={{0,1},{1,2},{2,3},{3,4},{4,5},{5,6},{6,7},{7,8},{8,9},{9,10},{10,1... | collective-permute-start | bytes 1044488 | tf_op jit(solution)/shard_map/ppermute | solution.py:282
  65.1 10.2 %collective-permute-start.15 = (f32[136,640]{1,0:T(8,128)S(1)}, f32[136,640]{1,0:T(8,128)S(1)}, u32[]{:S(2)}, u32[]{:S(2)}) collective-permute-start(f32[136,640]{1,0:T(8,128)S(1)} %get-tuple-element.43), channel_id=1, source_target_pairs={{1,0},{2,1},{3,2},{4,3},{5,4},{6,5},{7,6},{8,7},{9,8},{10,9},{11,1... | collective-permute-start | bytes 1044488 | tf_op jit(solution)/shard_map/ppermute | solution.py:283
  70.2 9.1 %collective-permute-start.12 = (f32[128,512]{1,0:T(8,128)S(1)}, f32[128,512]{1,0:T(8,128)S(1)}, u32[]{:S(2)}, u32[]{:S(2)}) collective-permute-start(f32[128,512]{1,0:T(8,128)S(1)} %get-tuple-element.40), channel_id=1, source_target_pairs={{0,1},{1,2},{2,3},{3,4},{4,5},{5,6},{6,7},{7,8},{8,9},{9,10},{10,1... | collective-permute-start | bytes 786440 | tf_op jit(solution)/shard_map/ppermute | solution.py:282
  70.2 9.1 %collective-permute-start.13 = (f32[128,512]{1,0:T(8,128)S(1)}, f32[128,512]{1,0:T(8,128)S(1)}, u32[]{:S(2)}, u32[]{:S(2)}) collective-permute-start(f32[128,512]{1,0:T(8,128)S(1)} %get-tuple-element.41), channel_id=1, source_target_pairs={{1,0},{2,1},{3,2},{4,3},{5,4},{6,5},{7,6},{8,7},{9,8},{10,9},{11,1... | collective-permute-start | bytes 786440 | tf_op jit(solution)/shard_map/ppermute | solution.py:283
where the time goes:
time: 84.3 us; the launch traced here: 83.8 us
  starting transfers between devices  41.1 us (49%)
  Pallas kernels  23.1 us (27%)
  local copies, waits for them, and re-layouts  10.3 us (12%)
  waiting for transfers between devices  6.27 us (7%)
  other arithmetic  2.33 us (3%)
    ppermute x7, starting transfers between devices, send_columns(): from_e = [lax.ppermute(m, 'comp', west) for m in messages[half:]]  38.5 us
    pallas_call x9, Pallas kernels, kernel_call(): pl.pallas_call(body, out_shape=[jax.ShapeDtypeStruct(shape, jnp.float32)...  23.1 us
    unnamed x23, local copies, waits for them, and re-layouts  7.51 us
    ppermute x7, waiting for transfers between devices, send_columns(): from_w = [lax.ppermute(m, 'comp', east) for m in messages[:half]]  6.24 us
    ppermute x1, starting transfers between devices, shards(): low = lax.ppermute(low, 'sec', up)  2.01 us
  transfers between devices with their start and end apart: 16, of which 4 were waited for; matrix products, arithmetic and copies ran while one was open for 8% of the time, Pallas kernels for 9%

commit v1 on v0

--- a/solution.py
+++ b/solution.py
@@ -15,6 +15,8 @@
 LAYERS = 40
 SUBSTEPS = 4
 STEPS = 3
+NLAT = 96
+BANDS = 4
 HALO = SUBSTEPS
 FAR = STEPS * HALO
 OWN = 6
@@ -65,10 +67,17 @@
     return sizes * 2
 
 
-def enter(spec, land, flow, ocean, state, low, high, square):
+def enter(*refs):
+    sources, (state, low, high, group_out, square), copies, sems = refs[:5], refs[5:10], refs[10:15], refs[15]
+    moves = [pltpu.make_async_copy(a, b, sems.at[i]) for i, (a, b) in enumerate(zip(sources, copies))]
+    for move in moves:
+        move.start()
+    spec, land, flow, ocean, group = copies
     rows = spec.shape[1]
     lane = lax.broadcasted_iota(jnp.int32, (rows, LANES), 1)
     square[...] = jnp.zeros_like(square)
+    for move in moves:
+        move.wait()
     square[:OWN, :rows] = land[...].astype(jnp.float32)
     for c in range(OWN):
         square[8 + c : 9 + c, :rows] = flow[c, 0:1]
@@ -87,10 +96,21 @@
         at = pl.ds(c * FAR, FAR)
         low[at] = state[c, rows - FAR :]
         high[at] = state[c, :FAR]
-
-
-def pack_own(state, east, west):
+    group_out[...] = group[...]
+
+
+def pack_own(state, group, east, west, speeds):
     rows = state.shape[1]
+    place = lax.broadcasted_iota(jnp.int32, (1, K), 1).astype(jnp.float32)
+    speed = jnp.zeros((1, K), jnp.float32)
+    turn = place
+    for f in range(FREQS):
+        later = place >= f * DIRS
+        speed = jnp.where(later, group[0:1, f : f + 1], speed)
+        turn = jnp.where(later, place - f * DIRS, turn)
+    theta = 2.0 * math.pi * (turn + 0.5) / DIRS
+    speeds[0:1] = speed * jnp.cos(theta)
+    speeds[1:2] = speed * jnp.sin(theta)
     for c in range(HALO):
         east[c * rows : (c + 1) * rows] = state[2 + c, :, :K]
         west[c * rows : (c + 1) * rows] = state[c, :, :K]
@@ -193,12 +213,12 @@
     refs = list(refs)
     take = lambda n: [refs.pop(0) for _ in range(n)]
     states, from_w, from_e = take(pieces), take(pieces), take(pieces)
-    (aux_w, aux_e, speeds, done, rate, mixing, w_gate, w_up, w_down, profile, state_out) = take(11)
+    (aux_w, aux_e, speeds, done, mixing, w_gate, w_up, w_down, profile, state_out) = take(10)
     if last:
         (ocean_out,) = take(1)
     else:
         messages = take(4)
-    act, hidden = take(2)
+    act, hidden, wide_profile, kappas = take(4)
     split = HALVES[1][0]
     fewer = rows - 2 * HALO
     advect(1, rows, pieces > 1, states, from_w, from_e, aux_w, aux_e, speeds, state_out, split, refs)
@@ -222,14 +242,23 @@
             fresh = mask * (old + source[c * fewer : (c + 1) * fewer])
             state_out[c, :, n : n + size] = fresh
             act[at, n : n + size] = fresh.astype(jnp.bfloat16)
-    stokes = jnp.dot(act[...], profile[...], preferred_element_type=jnp.float32)
+    layers = profile.shape[0]
+    wide_profile[:layers] = profile[...]
+    wide_profile[layers:] = jnp.zeros((LANES - layers, K), jnp.bfloat16)
+    stokes = lax.dot_general(
+        act[...], wide_profile[...], (((1,), (1,)), ((), ())), preferred_element_type=jnp.float32
+    )
 
     lane = lax.broadcasted_iota(jnp.int32, (fewer, LANES), 1)
     east = lane < LAYERS
-    kappa = mixing[...]
-    speed = rate[...]
-    for r in range(rate.shape[0], rows - 1, -2 * HALO):
-        speed = shrink(speed, r)
+    kappas[:, :LAYERS] = mixing[...]
+    kappas[:, LAYERS : 2 * LAYERS] = mixing[...]
+    kappa = kappas[...]
+    place = lax.broadcasted_iota(jnp.int32, (fewer, LANES), 0)
+    reach = (fewer - NLAT // BANDS) // 2
+    place = jnp.where(place < fewer - reach, place, place - fewer)
+    place = (lax.axis_index("sec") * (NLAT // BANDS) + place).astype(jnp.float32)
+    speed = 0.5 * jnp.sin((place + 0.5) * (math.pi / NLAT) - math.pi / 2)
     surf = []
     for c in range(OWN):
         v = shrink(jnp.concatenate([piece[c, :, K:] for piece in states], axis=0), rows)
@@ -253,12 +282,12 @@
             messages[2 * side][HALO * fewer :, :LANES] = tile
 
 
-def kernel_call(body, outs, scratch, *args, flops=0):
+def kernel_call(body, outs, scratch, *args, flops=0, space=pltpu.VMEM):
     block = pl.BlockSpec(memory_space=pltpu.VMEM)
     return pl.pallas_call(
         body,
         out_shape=[jax.ShapeDtypeStruct(shape, jnp.float32) for shape in outs],
-        in_specs=[block] * len(args),
+        in_specs=[pl.BlockSpec(memory_space=space)] * len(args),
         out_specs=[block] * len(outs),
         scratch_shapes=scratch,
         compiler_params=pltpu.CompilerParams(vmem_limit_bytes=14 << 20),
@@ -271,7 +300,6 @@
 ):
     rows, columns, _ = spectrum.shape
     bands, sectors = lax.axis_size("sec"), lax.axis_size("comp")
-    band = lax.axis_index("sec")
     up = [(i, (i + 1) % bands) for i in range(bands)]
     down = [(b, a) for a, b in up]
     east = [(i, (i + 1) % sectors) for i in range(sectors)]
@@ -284,29 +312,28 @@
         return [from_w[0], from_w[-1]], [from_e[0], from_e[-1]]
 
     edge = (columns * FAR, FULL)
-    state, low, high = kernel_call(
+    inputs = (
+        spectrum.transpose(1, 0, 2),
+        land.T,
+        currents.transpose(2, 0, 1),
+        ocean_vel.transpose(0, 3, 2, 1),
+        group_courant[None],
+    )
+    state, low, high, group = kernel_call(
         enter,
-        [(columns, rows, FULL), edge, edge],
-        [pltpu.VMEM((LANES, LANES), jnp.float32)],
-        spectrum.transpose(1, 0, 2), land.T, currents.transpose(2, 0, 1), ocean_vel.transpose(0, 3, 2, 1),
+        [(columns, rows, FULL), edge, edge, (1, FREQS)],
+        [pltpu.VMEM((LANES, LANES), jnp.float32)]
+        + [pltpu.VMEM(x.shape, x.dtype) for x in inputs]
+        + [pltpu.SemaphoreType.DMA((len(inputs),))],
+        *inputs,
+        space=pltpu.HBM,
     )
     low = lax.ppermute(low, "sec", up)
     high = lax.ppermute(high, "sec", down)
-    own = send_columns(kernel_call(pack_own, [(HALO * rows, K)] * 2, [], state))
-
+    side = (HALO * rows, K)
+    *messages, speeds = kernel_call(pack_own, [side, side, (8, K)], [], state, group)
+    own = send_columns(messages)
     tall = rows + 2 * FAR
-    places = jnp.concatenate([jnp.arange(rows + FAR), jnp.arange(-FAR, 0)])
-    places = (band * rows + places).astype(jnp.float32)
-    rate = 0.5 * jnp.sin((places + 0.5) * (math.pi / (rows * bands)) - math.pi / 2)
-    rate = jnp.broadcast_to(rate[:, None], (tall, LANES))
-
-    theta = 2.0 * math.pi * (jnp.arange(DIRS).astype(jnp.float32) + 0.5) / DIRS
-    speed = jnp.repeat(group_courant, DIRS)
-    speeds = jnp.stack([speed * jnp.tile(jnp.cos(theta), FREQS), speed * jnp.tile(jnp.sin(theta), FREQS)])
-    speeds = jnp.pad(speeds, ((0, 6), (0, 0)))
-    kappa = jnp.pad(jnp.concatenate([mixing, mixing]), (0, LANES - 2 * LAYERS))[None, :]
-    profile = jnp.pad(stokes_profile, ((0, 0), (0, LANES - 2 * LAYERS)))
-
     far, *messages = kernel_call(
         pack_far, [(columns, 2 * FAR, FULL), *message_shapes(2 * FAR)], [], state, low, high
     )
@@ -320,7 +347,10 @@
         scratch = [pltpu.VMEM(plane, jnp.float32)] * 5 + [
             pltpu.VMEM((2, EXT, tall + 16, LANES), jnp.float32),
         ]
-        matmul = [pltpu.VMEM((columns * fewer, K), jnp.bfloat16)] * 2
+        matmul = [pltpu.VMEM((columns * fewer, K), jnp.bfloat16)] * 2 + [
+            pltpu.VMEM((LANES, K), jnp.bfloat16),
+            pltpu.VMEM((1, LANES), jnp.float32),
+        ]
         from_w = [[a[0][half] for a in arrived] for half in range(2)]
         from_e = [[a[1][half] for a in arrived] for half in range(2)]
         (done,) = kernel_call(
@@ -339,7 +369,7 @@
             outs,
             matmul + scratch,
             *states, *from_w[1], *from_e[1], from_w[0][-1], from_e[0][-1],
-            speeds, done, rate, kappa, w_gate, w_up, w_down, profile,
+            speeds, done, mixing[None], w_gate, w_up, w_down, stokes_profile.T,
             flops=1 << 32,
         )
         if not last:

time: 84.3 us -> 77.2 us (0.916)
  local copies, waits for them, and re-layouts: 10.3 us -> 4.05 us
  other arithmetic: 2.33 us -> 0 us
  waiting for transfers between devices: 6.27 us -> 8.21 us
    unnamed x23 -> x20, local copies, waits for them, and re-layouts: 7.51 us -> 4.05 us
    mul x2 -> x0, local copies, waits for them, and re-layouts: 1.65 us -> none  [the longest x1 0.83 us: shards(): speed * jnp.tile(jnp.sin(theta), FREQS)]
    mul x2 -> x0, other arithmetic: 1.46 us -> none  [the longest x1 1.34 us: shards(): speed * jnp.tile(jnp.cos(theta), FREQS)]
    ppermute x1, waiting for transfers between devices: 0.01 us -> 1.3 us  [shards(): high = lax.ppermute(high, 'sec', down)]
    pad x1 -> x0, local copies, waits for them, and re-layouts: 1.02 us -> none  [shards(): profile = jnp.pad(stokes_profile, ((0, 0), (0, LANES - 2 * LAYERS)))]
  transfers between devices with their start and end apart: 16 -> 16, of which waited for: 4 -> 6; matrix products, arithmetic and copies ran while one was open for 8% -> 0% of each run, Pallas kernels for 9% -> 9%
where the time goes in v1:
time: 77.2 us; the launch traced here: 77 us
  starting transfers between devices  41.7 us (54%)
  Pallas kernels  22.3 us (29%)
  waiting for transfers between devices  8.21 us (11%)
  local copies, waits for them, and re-layouts  4.05 us (5%)
  between operations  0.8 us (1%)
    ppermute x7, starting transfers between devices, send_columns(): from_e = [lax.ppermute(m, 'comp', west) for m in messages[half:]]  39 us
    pallas_call x9, Pallas kernels, kernel_call(): pl.pallas_call(body, out_shape=[jax.ShapeDtypeStruct(shape, jnp.float32)...  22.3 us
    ppermute x7, waiting for transfers between devices, send_columns(): from_w = [lax.ppermute(m, 'comp', east) for m in messages[:half]]  6.04 us
    unnamed x20, local copies, waits for them, and re-layouts  4.05 us
    ppermute x1, starting transfers between devices, shards(): low = lax.ppermute(low, 'sec', up)  2.01 us
  transfers between devices with their start and end apart: 16, of which 6 were waited for; matrix products, arithmetic and copies ran while one was open for 0% of the time, Pallas kernels for 9%

profile of v1, /device:TPU:24, one launch (start us, length us, event | category | flops | bytes accessed | tf_op | source)
XLA Modules:
  0.0 77.0 jit_solution(13783714462317200097)
XLA Ops:
  0.6 1.1 %copy-done = f32[24,6,1152]{2,0,1:T(8,128)S(1)} copy-done((f32[24,6,1152]{2,0,1:T(8,128)S(1)}, f32[24,6,1152]{2,0,1:T(8,128)}, u32[]{:S(2)}) %copy-start) | copy-done | bytes 663576
  1.7 0.9 %copy-done.1 = f32[2,40,24,6]{1,2,3,0:T(8,128)S(1)} copy-done((f32[2,40,24,6]{1,2,3,0:T(8,128)S(1)}, f32[2,40,24,6]{1,2,3,0:T(8,128)}, u32[]{:S(2)}) %copy-start.1) | copy-done | bytes 46104
  2.6 0.7 copy-done.2
  3.3 0.7 copy-done.3
  4.0 0.7 copy-done.4
  4.7 0.8 %shard_map.113 = (f32[6,24,1280]{2,1,0:T(8,128)S(1)}, f32[72,1280]{1,0:T(8,128)S(1)}, f32[72,1280]{1,0:T(8,128)S(1)}, f32[1,32]{1,0:T(1,128)S(1)}) custom-call(f32[6,24,1152]{2,1,0:T(8,128)S(1)} %bitcast.9, s32[6,24]{1,0:T(8,128)S(1)} %bitcast.12, f32[6,2,24]{2,1,0:T(2,128)S(1)} %bitcast.11, f32[2,6,24,40]{3,2,1,0:T(8,128)S(1)} %bitcast.10, f32[1,32]{1,0:T(1,128)S(1)} %bitcast.13), custom_call_target="tpu_custom_call" | custom-call | bytes 1048576 | tf_op jit(solution)/shard_map/pallas_call | solution.py:287
  5.5 2.0 %collective-permute-start = (f32[72,1280]{1,0:T(8,128)S(1)}, f32[72,1280]{1,0:T(8,128)S(1)}, u32[]{:S(2)}, u32[]{:S(2)}) collective-permute-start(f32[72,1280]{1,0:T(8,128)S(1)} %get-tuple-element.27), channel_id=1, source_target_pairs={{0,64},{64,128},{128,192},{192,0},{1,65},{65,129},{129,193},{193,1... | collective-permute-start | bytes 1105928 | tf_op jit(solution)/shard_map/ppermute | solution.py:331
  7.5 0.1 collective-permute-start.1
  7.6 0.4 shard_map.115
  7.9 0.1 collective-permute-start.2
  8.0 7.0 %collective-permute-start.4 = (f32[96,1152]{1,0:T(8,128)S(1)}, f32[96,1152]{1,0:T(8,128)S(1)}, u32[]{:S(2)}, u32[]{:S(2)}) collective-permute-start(f32[96,1152]{1,0:T(8,128)S(1)} %get-tuple-element.33), channel_id=1, source_target_pairs={{1,0},{2,1},{3,2},{4,3},{5,4},{6,5},{7,6},{8,7},{9,8},{10,9},{11,1... | collective-permute-start | bytes 1327112 | tf_op jit(solution)/shard_map/ppermute | solution.py:311
  15.0 0.8 %collective-permute-done.low = f32[72,1280]{1,0:T(8,128)S(1)} collective-permute-done((f32[72,1280]{1,0:T(8,128)S(1)}, f32[72,1280]{1,0:T(8,128)S(1)}, u32[]{:S(2)}, u32[]{:S(2)}) %collective-permute-start) | collective-permute-done | bytes 368672 | tf_op jit(solution)/shard_map/ppermute | solution.py:331
  15.9 1.3 %collective-permute-done.1.high = f32[72,1280]{1,0:T(8,128)S(1)} collective-permute-done((f32[72,1280]{1,0:T(8,128)S(1)}, f32[72,1280]{1,0:T(8,128)S(1)}, u32[]{:S(2)}, u32[]{:S(2)}) %collective-permute-start.1) | collective-permute-done | bytes 368672 | tf_op jit(solution)/shard_map/ppermute | solution.py:332
  17.2 0.3 shard_map.114
  17.5 0.1 collective-permute-start.6
  17.6 6.6 %collective-permute-start.7 = (f32[104,640]{1,0:T(8,128)S(1)}, f32[104,640]{1,0:T(8,128)S(1)}, u32[]{:S(2)}, u32[]{:S(2)}) collective-permute-start(f32[104,640]{1,0:T(8,128)S(1)} %get-tuple-element.36), channel_id=1, source_target_pairs={{1,0},{2,1},{3,2},{4,3},{5,4},{6,5},{7,6},{8,7},{9,8},{10,9},{11,1... | collective-permute-start | bytes 798728 | tf_op jit(solution)/shard_map/ppermute | solution.py:311
  24.2 0.0 collective-permute-start.3
  24.2 0.0 collective-permute-done.2.refs_2_
  24.2 5.1 %collective-permute-start.5 = (f32[96,512]{1,0:T(8,128)S(1)}, f32[96,512]{1,0:T(8,128)S(1)}, u32[]{:S(2)}, u32[]{:S(2)}) collective-permute-start(f32[96,512]{1,0:T(8,128)S(1)} %get-tuple-element.34), channel_id=1, source_target_pairs={{1,0},{2,1},{3,2},{4,3},{5,4},{6,5},{7,6},{8,7},{9,8},{10,9},{11,1... | collective-permute-start | bytes 589832 | tf_op jit(solution)/shard_map/ppermute | solution.py:311
  29.2 0.0 collective-permute-done.4.refs_4_
  29.2 0.0 collective-permute-done.6.refs_3_.refs_6_
  29.3 0.0 collective-permute-done.7.refs_5_.refs_7_
  29.3 0.0 copy-start.5
  29.3 0.0 copy-start.6
  29.3 0.0 copy-start.8
  29.3 0.0 copy-start.9
  29.3 2.4 %shard_map.116.refs_9_ = f32[6,40,640]{2,1,0:T(8,128)S(1)} custom-call(f32[6,24,1280]{2,1,0:T(8,128)S(1)} %get-tuple-element.26.own.state.refs_0_, f32[6,24,1280]{2,1,0:T(8,128)S(1)} %get-tuple-element.29.refs_1_, f32[96,1152]{1,0:T(8,128)S(1)} %collective-permute-done.2.refs_2_, f32[104,640]{1,0:T(8,128)S(1)} %collective-permute-done.6.refs_3_.refs_6_, ...), custom_call_target="tpu_custom_call" | custom-call | flops 2147483648 | bytes 1048576 | tf_op jit(solution)/shard_map/pallas_call | solution.py:287
  31.7 0.9 %collective-permute-done.3.refs_3_ = f32[96,512]{1,0:T(8,128)S(1)} collective-permute-done((f32[96,512]{1,0:T(8,128)S(1)}, f32[96,512]{1,0:T(8,128)S(1)}, u32[]{:S(2)}, u32[]{:S(2)}) %collective-permute-start.3) | collective-permute-done | bytes 196640 | tf_op jit(solution)/shard_map/ppermute | solution.py:310
  32.6 5.6 %shard_map.117 = (f32[6,40,1280]{2,1,0:T(8,128)S(1)}, f32[168,640]{1,0:T(8,128)S(1)}, f32[160,512]{1,0:T(8,128)S(1)}, f32[168,640]{1,0:T(8,128)S(1)}, f32[160,512]{1,0:T(8,128)S(1)}) custom-call(f32[6,24,1280]{2,1,0:T(8,128)S(1)} %get-tuple-element.26.own.state.refs_0_, f32[6,24,1280]{2,1,0:T(8,128)S(1)} %get-tuple-element.29.refs_1_, ...), custom_call_target="tpu_custom_call" | custom-call | flops 4294967296 | bytes 1048576 | tf_op jit(solution)/shard_map/pallas_call | solution.py:287
  38.3 0.3 collective-permute-start.10
  38.6 5.1 %collective-permute-start.11 = (f32[168,640]{1,0:T(8,128)S(1)}, f32[168,640]{1,0:T(8,128)S(1)}, u32[]{:S(2)}, u32[]{:S(2)}) collective-permute-start(f32[168,640]{1,0:T(8,128)S(1)} %get-tuple-element.42), channel_id=1, source_target_pairs={{1,0},{2,1},{3,2},{4,3},{5,4},{6,5},{7,6},{8,7},{9,8},{10,9},{11,1... | collective-permute-start | bytes 1290248 | tf_op jit(solution)/shard_map/ppermute | solution.py:311
  43.7 0.0 collective-permute-start.8
  43.7 5.1 %collective-permute-start.9 = (f32[160,512]{1,0:T(8,128)S(1)}, f32[160,512]{1,0:T(8,128)S(1)}, u32[]{:S(2)}, u32[]{:S(2)}) collective-permute-start(f32[160,512]{1,0:T(8,128)S(1)} %get-tuple-element.40), channel_id=1, source_target_pairs={{1,0},{2,1},{3,2},{4,3},{5,4},{6,5},{7,6},{8,7},{9,8},{10,9},{11,1... | collective-permute-start | bytes 983048 | tf_op jit(solution)/shard_map/ppermute | solution.py:311
  48.8 0.7 collective-permute-done.10.refs_1_.refs_3_
  49.5 0.0 collective-permute-done.11.refs_2_.refs_4_
  49.5 2.0 %shard_map.118.refs_6_ = f32[6,32,640]{2,1,0:T(8,128)S(1)} custom-call(f32[6,40,1280]{2,1,0:T(8,128)S(1)} %get-tuple-element.38.refs_0_, f32[168,640]{1,0:T(8,128)S(1)} %collective-permute-done.10.refs_1_.refs_3_, f32[168,640]{1,0:T(8,128)S(1)} %collective-permute-done.11.refs_2_.refs_4_, f32[8,1152]{1,0:T(8,128)S(1)} %get-tuple-element.37.refs_6_.refs_8_.refs_3_.refs_5_), custom_call_target="tpu_custom_call" | custom-call | flops 2147483648 | bytes 1048576 | tf_op jit(solution)/shard_map/pallas_call | solution.py:287
  51.5 2.0 %collective-permute-done.8.refs_1_ = f32[160,512]{1,0:T(8,128)S(1)} collective-permute-done((f32[160,512]{1,0:T(8,128)S(1)}, f32[160,512]{1,0:T(8,128)S(1)}, u32[]{:S(2)}, u32[]{:S(2)}) %collective-permute-start.8) | collective-permute-done | bytes 327712 | tf_op jit(solution)/shard_map/ppermute | solution.py:310
  53.5 0.0 collective-permute-done.9.refs_2_
  53.5 4.7 %shard_map.119 = (f32[6,32,1280]{2,1,0:T(8,128)S(1)}, f32[136,640]{1,0:T(8,128)S(1)}, f32[128,512]{1,0:T(8,128)S(1)}, f32[136,640]{1,0:T(8,128)S(1)}, f32[128,512]{1,0:T(8,128)S(1)}) custom-call(f32[6,40,1280]{2,1,0:T(8,128)S(1)} %get-tuple-element.38.refs_0_, f32[160,512]{1,0:T(8,128)S(1)} %collective-permute-done.8.refs_1_, ...), custom_call_target="tpu_custom_call" | custom-call | flops 4294967296 | bytes 1048576 | tf_op jit(solution)/shard_map/pallas_call | solution.py:287
  58.2 0.1 collective-permute-start.14
  58.3 5.1 %collective-permute-start.15 = (f32[136,640]{1,0:T(8,128)S(1)}, f32[136,640]{1,0:T(8,128)S(1)}, u32[]{:S(2)}, u32[]{:S(2)}) collective-permute-start(f32[136,640]{1,0:T(8,128)S(1)} %get-tuple-element.47), channel_id=1, source_target_pairs={{1,0},{2,1},{3,2},{4,3},{5,4},{6,5},{7,6},{8,7},{9,8},{10,9},{11,1... | collective-permute-start | bytes 1044488 | tf_op jit(solution)/shard_map/ppermute | solution.py:311
  63.5 5.1 %collective-permute-start.13 = (f32[128,512]{1,0:T(8,128)S(1)}, f32[128,512]{1,0:T(8,128)S(1)}, u32[]{:S(2)}, u32[]{:S(2)}) collective-permute-start(f32[128,512]{1,0:T(8,128)S(1)} %get-tuple-element.45), channel_id=1, source_target_pairs={{1,0},{2,1},{3,2},{4,3},{5,4},{6,5},{7,6},{8,7},{9,8},{10,9},{11,1... | collective-permute-start | bytes 786440 | tf_op jit(solution)/shard_map/ppermute | solution.py:311
  68.5 0.0 collective-permute-done.14.refs_1_.refs_3_
  68.5 0.0 collective-permute-done.15.refs_2_.refs_4_
  68.5 1.6 %shard_map.120.refs_6_ = f32[6,24,640]{2,1,0:T(8,128)S(1)} custom-call(f32[6,32,1280]{2,1,0:T(8,128)S(1)} %get-tuple-element.43.refs_0_, f32[136,640]{1,0:T(8,128)S(1)} %collective-permute-done.14.refs_1_.refs_3_, f32[136,640]{1,0:T(8,128)S(1)} %collective-permute-done.15.refs_2_.refs_4_, f32[8,1152]{1,0:T(8,128)S(1)} %get-tuple-element.37.refs_6_.refs_8_.refs_3_.refs_5_), custom_call_target="tpu_custom_call" | custom-call | flops 2147483648 | bytes 1048576 | tf_op jit(solution)/shard_map/pallas_call | solution.py:287
  70.1 2.5 %collective-permute-done.12.refs_1_ = f32[128,512]{1,0:T(8,128)S(1)} collective-permute-done((f32[128,512]{1,0:T(8,128)S(1)}, f32[128,512]{1,0:T(8,128)S(1)}, u32[]{:S(2)}, u32[]{:S(2)}) %collective-permute-start.12) | collective-permute-done | bytes 262176 | tf_op jit(solution)/shard_map/ppermute | solution.py:310
  72.6 0.0 collective-permute-done.13.refs_2_
  72.6 4.4 %shard_map.121 = (f32[6,24,1152]{2,1,0:T(8,128)}, f32[2,6,24,40]{3,2,1,0:T(8,128)}) custom-call(f32[6,32,1280]{2,1,0:T(8,128)S(1)} %get-tuple-element.43.refs_0_, f32[128,512]{1,0:T(8,128)S(1)} %collective-permute-done.12.refs_1_, f32[128,512]{1,0:T(8,128)S(1)} %collective-permute-done.13.refs_2_, f32[136,640]{1,0:T(8,128)S(1)} %collective-permute-done.14.refs_1_.refs_3_, ...), custom_call_target="tpu_custom_call" | custom-call | flops 4294967296 | bytes 1048576 | tf_op jit(solution)/shard_map/pallas_call | solution.py:287
  (13 shorter events, 0.0 us)
Async XLA Ops:
  0.6 1.1 %copy-start = (f32[24,6,1152]{2,0,1:T(8,128)S(1)}, f32[24,6,1152]{2,0,1:T(8,128)}, u32[]{:S(2)}) copy-start(f32[24,6,1152]{2,0,1:T(8,128)} %param.10) | copy-start | bytes 1990660
  1.7 0.9 %copy-start.1 = (f32[2,40,24,6]{1,2,3,0:T(8,128)S(1)}, f32[2,40,24,6]{1,2,3,0:T(8,128)}, u32[]{:S(2)}) copy-start(f32[2,40,24,6]{1,2,3,0:T(8,128)} %param.18) | copy-start | bytes 138244
  2.6 0.7 copy-start.2
  3.3 0.7 copy-start.3
  4.0 0.7 copy-start.4
  5.5 10.4 %collective-permute-start = (f32[72,1280]{1,0:T(8,128)S(1)}, f32[72,1280]{1,0:T(8,128)S(1)}, u32[]{:S(2)}, u32[]{:S(2)}) collective-permute-start(f32[72,1280]{1,0:T(8,128)S(1)} %get-tuple-element.27), channel_id=1, source_target_pairs={{0,64},{64,128},{128,192},{192,0},{1,65},{65,129},{129,193},{193,1... | collective-permute-start | bytes 1105928 | tf_op jit(solution)/shard_map/ppermute | solution.py:331
  7.5 9.7 %collective-permute-start.1 = (f32[72,1280]{1,0:T(8,128)S(1)}, f32[72,1280]{1,0:T(8,128)S(1)}, u32[]{:S(2)}, u32[]{:S(2)}) collective-permute-start(f32[72,1280]{1,0:T(8,128)S(1)} %get-tuple-element.28), channel_id=1, source_target_pairs={{64,0},{128,64},{192,128},{0,192},{65,1},{129,65},{193,129},{1,193... | collective-permute-start | bytes 1105928 | tf_op jit(solution)/shard_map/ppermute | solution.py:332
  7.9 16.3 %collective-permute-start.2 = (f32[96,1152]{1,0:T(8,128)S(1)}, f32[96,1152]{1,0:T(8,128)S(1)}, u32[]{:S(2)}, u32[]{:S(2)}) collective-permute-start(f32[96,1152]{1,0:T(8,128)S(1)} %get-tuple-element.31), channel_id=1, source_target_pairs={{0,1},{1,2},{2,3},{3,4},{4,5},{5,6},{6,7},{7,8},{8,9},{9,10},{10,1... | collective-permute-start | bytes 1327112 | tf_op jit(solution)/shard_map/ppermute | solution.py:310
  8.0 21.2 %collective-permute-start.4 = (f32[96,1152]{1,0:T(8,128)S(1)}, f32[96,1152]{1,0:T(8,128)S(1)}, u32[]{:S(2)}, u32[]{:S(2)}) collective-permute-start(f32[96,1152]{1,0:T(8,128)S(1)} %get-tuple-element.33), channel_id=1, source_target_pairs={{1,0},{2,1},{3,2},{4,3},{5,4},{6,5},{7,6},{8,7},{9,8},{10,9},{11,1... | collective-permute-start | bytes 1327112 | tf_op jit(solution)/shard_map/ppermute | solution.py:311
  17.2 15.4 %copy-start.7 = (bf16[1152,1152]{1,0:T(8,128)(2,1)S(1)}, bf16[1152,1152]{1,0:T(8,128)(2,1)}, u32[]{:S(2)}) copy-start(bf16[1152,1152]{1,0:T(8,128)(2,1)} %refs_10_.3) | copy-start | bytes 7962628
  17.5 11.7 %collective-permute-start.6 = (f32[104,640]{1,0:T(8,128)S(1)}, f32[104,640]{1,0:T(8,128)S(1)}, u32[]{:S(2)}, u32[]{:S(2)}) collective-permute-start(f32[104,640]{1,0:T(8,128)S(1)} %get-tuple-element.35), channel_id=1, source_target_pairs={{0,1},{1,2},{2,3},{3,4},{4,5},{5,6},{6,7},{7,8},{8,9},{9,10},{10,1... | collective-permute-start | bytes 798728 | tf_op jit(solution)/shard_map/ppermute | solution.py:310
  17.6 11.7 %collective-permute-start.7 = (f32[104,640]{1,0:T(8,128)S(1)}, f32[104,640]{1,0:T(8,128)S(1)}, u32[]{:S(2)}, u32[]{:S(2)}) collective-permute-start(f32[104,640]{1,0:T(8,128)S(1)} %get-tuple-element.36), channel_id=1, source_target_pairs={{1,0},{2,1},{3,2},{4,3},{5,4},{6,5},{7,6},{8,7},{9,8},{10,9},{11,1... | collective-permute-start | bytes 798728 | tf_op jit(solution)/shard_map/ppermute | solution.py:311
  24.2 8.4 %collective-permute-start.3 = (f32[96,512]{1,0:T(8,128)S(1)}, f32[96,512]{1,0:T(8,128)S(1)}, u32[]{:S(2)}, u32[]{:S(2)}) collective-permute-start(f32[96,512]{1,0:T(8,128)S(1)} %get-tuple-element.32), channel_id=1, source_target_pairs={{0,1},{1,2},{2,3},{3,4},{4,5},{5,6},{6,7},{7,8},{8,9},{9,10},{10,1... | collective-permute-start | bytes 589832 | tf_op jit(solution)/shard_map/ppermute | solution.py:310
  24.2 8.4 %collective-permute-start.5 = (f32[96,512]{1,0:T(8,128)S(1)}, f32[96,512]{1,0:T(8,128)S(1)}, u32[]{:S(2)}, u32[]{:S(2)}) collective-permute-start(f32[96,512]{1,0:T(8,128)S(1)} %get-tuple-element.34), channel_id=1, source_target_pairs={{1,0},{2,1},{3,2},{4,3},{5,4},{6,5},{7,6},{8,7},{9,8},{10,9},{11,1... | collective-permute-start | bytes 589832 | tf_op jit(solution)/shard_map/ppermute | solution.py:311
  29.3 3.3 %copy-start.5 = (bf16[1152,1152]{1,0:T(8,128)(2,1)S(1)}, bf16[1152,1152]{1,0:T(8,128)(2,1)}, u32[]{:S(2)}) copy-start(bf16[1152,1152]{1,0:T(8,128)(2,1)} %refs_8_.3) | copy-start | bytes 7962628
  29.3 3.3 %copy-start.6 = (bf16[1152,1152]{1,0:T(8,128)(2,1)S(1)}, bf16[1152,1152]{1,0:T(8,128)(2,1)}, u32[]{:S(2)}) copy-start(bf16[1152,1152]{1,0:T(8,128)(2,1)} %refs_9_.3) | copy-start | bytes 7962628
  29.3 3.3 %copy-start.8 = (bf16[1152,80]{0,1:T(8,128)(2,1)S(1)}, bf16[1152,80]{0,1:T(8,128)(2,1)}, u32[]{:S(2)}) copy-start(bf16[1152,80]{0,1:T(8,128)(2,1)} %param.17) | copy-start | bytes 552964
  29.3 3.3 %copy-start.9 = (f32[40]{0:T(128)S(1)}, f32[40]{0:T(128)}, u32[]{:S(2)}) copy-start(f32[40]{0:T(128)} %param.19) | copy-start | bytes 484
  38.3 11.2 %collective-permute-start.10 = (f32[168,640]{1,0:T(8,128)S(1)}, f32[168,640]{1,0:T(8,128)S(1)}, u32[]{:S(2)}, u32[]{:S(2)}) collective-permute-start(f32[168,640]{1,0:T(8,128)S(1)} %get-tuple-element.41), channel_id=1, source_target_pairs={{0,1},{1,2},{2,3},{3,4},{4,5},{5,6},{6,7},{7,8},{8,9},{9,10},{10,1... | collective-permute-start | bytes 1290248 | tf_op jit(solution)/shard_map/ppermute | solution.py:310
  38.6 10.9 %collective-permute-start.11 = (f32[168,640]{1,0:T(8,128)S(1)}, f32[168,640]{1,0:T(8,128)S(1)}, u32[]{:S(2)}, u32[]{:S(2)}) collective-permute-start(f32[168,640]{1,0:T(8,128)S(1)} %get-tuple-element.42), channel_id=1, source_target_pairs={{1,0},{2,1},{3,2},{4,3},{5,4},{6,5},{7,6},{8,7},{9,8},{10,9},{11,1... | collective-permute-start | bytes 1290248 | tf_op jit(solution)/shard_map/ppermute | solution.py:311
  43.7 9.8 %collective-permute-start.8 = (f32[160,512]{1,0:T(8,128)S(1)}, f32[160,512]{1,0:T(8,128)S(1)}, u32[]{:S(2)}, u32[]{:S(2)}) collective-permute-start(f32[160,512]{1,0:T(8,128)S(1)} %get-tuple-element.39), channel_id=1, source_target_pairs={{0,1},{1,2},{2,3},{3,4},{4,5},{5,6},{6,7},{7,8},{8,9},{9,10},{10,1... | collective-permute-start | bytes 983048 | tf_op jit(solution)/shard_map/ppermute | solution.py:310
  43.7 9.8 %collective-permute-start.9 = (f32[160,512]{1,0:T(8,128)S(1)}, f32[160,512]{1,0:T(8,128)S(1)}, u32[]{:S(2)}, u32[]{:S(2)}) collective-permute-start(f32[160,512]{1,0:T(8,128)S(1)} %get-tuple-element.40), channel_id=1, source_target_pairs={{1,0},{2,1},{3,2},{4,3},{5,4},{6,5},{7,6},{8,7},{9,8},{10,9},{11,1... | collective-permute-start | bytes 983048 | tf_op jit(solution)/shard_map/ppermute | solution.py:311
  58.2 10.3 %collective-permute-start.14 = (f32[136,640]{1,0:T(8,128)S(1)}, f32[136,640]{1,0:T(8,128)S(1)}, u32[]{:S(2)}, u32[]{:S(2)}) collective-permute-start(f32[136,640]{1,0:T(8,128)S(1)} %get-tuple-element.46), channel_id=1, source_target_pairs={{0,1},{1,2},{2,3},{3,4},{4,5},{5,6},{6,7},{7,8},{8,9},{9,10},{10,1... | collective-permute-start | bytes 1044488 | tf_op jit(solution)/shard_map/ppermute | solution.py:310
  58.3 10.2 %collective-permute-start.15 = (f32[136,640]{1,0:T(8,128)S(1)}, f32[136,640]{1,0:T(8,128)S(1)}, u32[]{:S(2)}, u32[]{:S(2)}) collective-permute-start(f32[136,640]{1,0:T(8,128)S(1)} %get-tuple-element.47), channel_id=1, source_target_pairs={{1,0},{2,1},{3,2},{4,3},{5,4},{6,5},{7,6},{8,7},{9,8},{10,9},{11,1... | collective-permute-start | bytes 1044488 | tf_op jit(solution)/shard_map/ppermute | solution.py:311
  63.5 9.1 %collective-permute-start.12 = (f32[128,512]{1,0:T(8,128)S(1)}, f32[128,512]{1,0:T(8,128)S(1)}, u32[]{:S(2)}, u32[]{:S(2)}) collective-permute-start(f32[128,512]{1,0:T(8,128)S(1)} %get-tuple-element.44), channel_id=1, source_target_pairs={{0,1},{1,2},{2,3},{3,4},{4,5},{5,6},{6,7},{7,8},{8,9},{9,10},{10,1... | collective-permute-start | bytes 786440 | tf_op jit(solution)/shard_map/ppermute | solution.py:310
  63.5 9.1 %collective-permute-start.13 = (f32[128,512]{1,0:T(8,128)S(1)}, f32[128,512]{1,0:T(8,128)S(1)}, u32[]{:S(2)}, u32[]{:S(2)}) collective-permute-start(f32[128,512]{1,0:T(8,128)S(1)} %get-tuple-element.45), channel_id=1, source_target_pairs={{1,0},{2,1},{3,2},{4,3},{5,4},{6,5},{7,6},{8,7},{9,8},{10,9},{11,1... | collective-permute-start | bytes 786440 | tf_op jit(solution)/shard_map/ppermute | solution.py:311
